TPU v7x, 32 devices: a whole 2x2x4 slice. The times are simulated.
32 devices in a mesh: expert: 8 (over z, core), hidden: 4 (over y, x).
Axes of the slice: x: 2, y: 2, z: 4, core: 2. Of those that a mesh axis runs over, the one named last changes fastest.
Arguments:
- inputs: bfloat16 [1536, 2880], P('expert', 'hidden'), may hold values from -6 to 6
- out_grad: bfloat16 [1536, 2880], P('expert', 'hidden'), may hold values from -6 to 6
- expert_ids: int32 [1536, 4], P('expert'), may hold values from 0 to 7, all different within a row; in each aligned block of 192 rows (0 to 191, 192 to 383, ...) at most 144 rows name the same one
- route_weight: float32 [1536, 4], P('expert'), may hold values from 0.1 to 1
- w_gate: bfloat16 [8, 2880, 2880], P('expert', 'hidden'), may hold values from -0.109375 to 0.109375
- w_up: bfloat16 [8, 2880, 2880], P('expert', 'hidden'), may hold values from -0.109375 to 0.109375
- w_down: bfloat16 [8, 2880, 2880], P('expert', 'hidden'), may hold values from -0.109375 to 0.109375
Outputs:
- grad_input: bfloat16 [1536, 2880], P('expert', 'hidden')
- grad_route: float32 [1536, 4], P('expert')
- grad_gate: float32 [8, 2880, 2880], P('expert', 'hidden')
- grad_up: float32 [8, 2880, 2880], P('expert', 'hidden')
- grad_down: float32 [8, 2880, 2880], P('expert', 'hidden')
Inputs may be any that keep to these rules, and one draw needn't show every extreme that they name: `expert_ids`: each token names 4 different experts. Among the 192 tokens of one index of the expert axis no expert is named more than 144 times, a bound that some block reaches.
All inputs are finite; a program needn't handle non-finite values.
Results may differ from a plain program's by a relative error of at most 0.018.
Values may be sent and summed in bfloat16 or wider, within the bound.
No kernel may reach another device: no remote copies, remote signals or barrier semaphores. Data moves between devices by JAX's collectives and lax.ppermute only.
A program may use at most 128 MiB of HBM per device.

v0:
```python
import jax
import jax.numpy as jnp
from jax import lax
from jax.sharding import PartitionSpec as P


def slot_tables(expert_ids, experts, capacity):
    count, top = expert_ids.shape
    flat = expert_ids.reshape(-1)
    onehot = (flat[:, None] == jnp.arange(experts, dtype=jnp.int32)[None, :]).astype(jnp.int32)
    position = jnp.cumsum(onehot, axis=0) - 1
    slot = jnp.sum(onehot * position, axis=1)
    dest = flat * capacity + slot
    table = (
        jnp.zeros((experts * capacity,), jnp.int32)
        .at[dest]
        .set(jnp.arange(count * top, dtype=jnp.int32))
    )
    filled = jnp.zeros((experts * capacity,), jnp.int32).at[dest].set(1)
    return (dest, table, filled)


def pack_rows(values, table, filled, top, experts, capacity):
    picked = values[table // top] * filled.astype(values.dtype)[:, None]
    return picked.reshape(experts, capacity, values.shape[1])


def to_local(buffer, n_groups, local_count):
    rest = buffer.shape[2:]
    shaped = buffer.reshape((n_groups, local_count, buffer.shape[1]) + rest)
    return jnp.swapaxes(shaped, 0, 1).reshape((local_count, n_groups * buffer.shape[1]) + rest)


def from_local(buffer, n_groups, capacity):
    local_count = buffer.shape[0]
    rest = buffer.shape[2:]
    shaped = buffer.reshape((local_count, n_groups, capacity) + rest)
    return jnp.swapaxes(shaped, 0, 1).reshape((n_groups * local_count, capacity) + rest)


def per_device(inputs, out_grad, expert_ids, route_weight, w_gate, w_up, w_down):
    n_groups = lax.axis_size("expert")
    local_count = w_gate.shape[0]
    experts = local_count * n_groups
    tok_count, top = expert_ids.shape
    capacity = 3 * top * tok_count // (2 * experts)
    dest, table, filled = slot_tables(expert_ids, experts, capacity)
    send_weight = (route_weight.reshape(-1)[table] * filled.astype(jnp.float32)).reshape(
        experts, capacity
    )
    send_x = pack_rows(inputs, table, filled, top, experts, capacity)
    send_dy = pack_rows(out_grad, table, filled, top, experts, capacity)
    got_x, got_dy, got_weight = (
        lax.all_to_all(send_x, "expert", split_axis=0, concat_axis=0, tiled=True),
        lax.all_to_all(send_dy, "expert", split_axis=0, concat_axis=0, tiled=True),
        lax.all_to_all(
            send_weight.astype(jnp.bfloat16), "expert", split_axis=0, concat_axis=0, tiled=True
        ).astype(send_weight.dtype),
    )
    rows_x, rows_dy = (
        lax.all_gather(got_x, "hidden", axis=2, tiled=True),
        lax.all_gather(got_dy, "hidden", axis=2, tiled=True),
    )
    xs = to_local(rows_x, n_groups, local_count)
    dys = to_local(rows_dy, n_groups, local_count)
    weights = to_local(got_weight, n_groups, local_count)
    gate = jnp.einsum("esd,efd->esf", xs, w_gate, preferred_element_type=jnp.float32)
    up = jnp.einsum("esd,efd->esf", xs, w_up, preferred_element_type=jnp.float32)
    sig = jax.nn.sigmoid(gate)
    act = gate * sig
    hidden = (act * up).astype(jnp.bfloat16)
    back = jnp.einsum("esd,efd->esf", dys, w_down, preferred_element_type=jnp.float32)
    route_part = jnp.sum(hidden.astype(jnp.float32) * back, axis=2)
    grad_hidden = weights[:, :, None] * back
    scaled = (weights[:, :, None] * dys.astype(jnp.float32)).astype(jnp.bfloat16)
    grad_down = jnp.einsum("esf,esd->efd", hidden, scaled, preferred_element_type=jnp.float32)
    d_gate = (grad_hidden * up * sig * (1.0 + gate * (1.0 - sig))).astype(jnp.bfloat16)
    d_up = (grad_hidden * act).astype(jnp.bfloat16)
    grad_gate = jnp.einsum("esf,esd->efd", d_gate, xs, preferred_element_type=jnp.float32)
    grad_up = jnp.einsum("esf,esd->efd", d_up, xs, preferred_element_type=jnp.float32)
    partial_value = jnp.einsum("esf,efd->esd", d_gate, w_gate, preferred_element_type=jnp.float32)
    partial_value = partial_value + jnp.einsum(
        "esf,efd->esd", d_up, w_up, preferred_element_type=jnp.float32
    )
    route_total = lax.psum(route_part, "hidden")
    route_back = from_local(route_total, n_groups, capacity)
    summed = lax.psum_scatter(
        partial_value.astype(jnp.bfloat16), "hidden", scatter_dimension=2, tiled=True
    ).astype(jnp.float32)
    back_rows, back_route = (
        lax.all_to_all(
            from_local(summed, n_groups, capacity).astype(jnp.bfloat16),
            "expert",
            split_axis=0,
            concat_axis=0,
            tiled=True,
        ).astype(jnp.float32),
        lax.all_to_all(
            route_back.astype(jnp.bfloat16), "expert", split_axis=0, concat_axis=0, tiled=True
        ).astype(route_back.dtype),
    )
    per_pair = back_rows.reshape(experts * capacity, back_rows.shape[2])[dest]
    grad_input = jnp.sum(per_pair.reshape(tok_count, top, per_pair.shape[1]), axis=1).astype(
        jnp.bfloat16
    )
    grad_route = back_route.reshape(-1)[dest].reshape(tok_count, top)
    return (grad_input, grad_route, grad_gate, grad_up, grad_down)


def solution(mesh):
    placed = (
        P("expert", "hidden"),
        P("expert", "hidden"),
        P("expert", None),
        P("expert", None),
        P("expert", "hidden", None),
        P("expert", "hidden", None),
        P("expert", "hidden", None),
    )
    return jax.shard_map(
        per_device,
        mesh=mesh,
        in_specs=placed,
        out_specs=(
            P("expert", "hidden"),
            P("expert", None),
            P("expert", "hidden", None),
            P("expert", "hidden", None),
            P("expert", "hidden", None),
        ),
        check_vma=False,
    )
```

profile of v0, /device:TPU:0, one launch (start us, length us, event | category | flops | bytes accessed | tf_op | source)
XLA Modules:
  0.0 514.7 jit_solution(17609842924973014855)
XLA Ops:
  7.2 0.0 copy-start
  7.2 0.0 all-gather.5.cloned.1.call-start
  7.2 0.8 copy.50
  8.1 0.1 eq.29
  8.2 0.1 eq.25
  8.3 0.7 broadcast_multiply_fusion.2
  9.0 1.7 reduce-window.6
  10.7 0.1 slice.18
  10.8 0.1 copy.52
  10.9 0.2 reduce-window.9
  11.1 0.1 copy.53
  11.1 0.1 copy.49
  11.3 0.1 mul.98
  11.4 0.1 fusion.15
  11.5 3.4 scatter_custom_fusion
  15.0 0.0 copy-start.2
  15.0 4.6 gather_fusion.1
  19.5 4.8 gather_fusion.2
  24.4 3.4 scatter_custom_fusion.1
  27.8 0.1 mul.102
  27.9 3.0 broadcast_multiply_fusion.1
  30.8 48.3 %all_to_all.27 = bf16[8,144,720]{2,1,0:T(8,128)(2,1)} all-to-all(bf16[8,144,720]{2,1,0:T(8,128)(2,1)S(1)} %get-tuple-element.32), channel_id=1, replica_groups=mesh['expert'=8,'hidden'=4] {'expert'}, dimensions={0} | all-to-all | bytes 3317760 | tf_op jit(solution)/shard_map/all_to_all | solution.py:54
  79.1 5.1 copy.57
  84.2 0.0 all-gather.5.cloned.1.call-update
  84.2 0.0 all-gather.3.cloned.1.call-start
  84.3 45.2 %all_to_all.28 = bf16[8,144,720]{2,1,0:T(8,128)(2,1)} all-to-all(bf16[8,144,720]{2,1,0:T(8,128)(2,1)S(1)} %copy-done.3), channel_id=1, replica_groups=mesh['expert'=8,'hidden'=4] {'expert'}, dimensions={0} | all-to-all | bytes 3317760 | tf_op jit(solution)/shard_map/all_to_all | solution.py:55
  129.4 5.0 copy.55
  134.4 0.0 all-gather.3.cloned.1.call-update
  134.5 0.0 reduce-scatter.7.cloned.1.call-start
  134.5 0.1 copy.48
  134.6 0.1 reshape.221
  134.8 4.6 gather_fusion
  139.3 0.1 convert_element_type.129
  139.4 8.0 %all_to_all.29 = bf16[8,1,144]{2,1,0:T(2,128)(2,1)S(1)} all-to-all(bf16[8,1,144]{2,1,0:T(2,128)(2,1)S(1)} %convert_element_type.129), channel_id=1, replica_groups=mesh['expert'=8,'hidden'=4] {'expert'}, dimensions={0} | all-to-all | bytes 4608 | tf_op jit(solution)/shard_map/all_to_all | solution.py:56
  147.4 0.1 reshape.232
  147.5 51.6 %all-gather.5.cloned.1.call-done = bf16[8,144,2880]{1,0,2:T(8,128)(2,1)} async-done(((bf16[8,144,720]{1,0,2:T(8,128)(2,1)}), bf16[8,144,2880]{1,0,2:T(8,128)(2,1)}) %all-gather.5.cloned.1.call-update) | async-done | bytes 6635536 | tf_op jit(solution)/shard_map/all_gather | solution.py:61
  199.1 16.3 %copy.58 = bf16[8,144,2880]{2,1,0:T(8,128)(2,1)} copy(bf16[8,144,2880]{1,0,2:T(8,128)(2,1)} %all-gather.5.cloned.1.call-done) | data formatting | bytes 13271040 | tf_op jit(solution)/shard_map/all_gather | solution.py:61
  215.4 11.0 %fusion.10 = f32[1152,720]{0,1:T(8,128)} fusion(bf16[1152,2880]{1,0:T(8,128)(2,1)} %bitcast.60, bf16[1,720,2880]{2,1,0:T(8,128)(2,1)} %param.12), kind=kOutput, calls=%fused_computation.21 | convolution fusion | flops 4777574400 | bytes 14100480 | tf_op jit(solution)/shard_map/esd,efd->esf/dot_general | solution.py:68
  226.4 7.6 %fusion.7 = f32[1152,720]{0,1:T(8,128)} fusion(bf16[1152,2880]{1,0:T(8,128)(2,1)S(1)} %bitcast.63, bf16[1,720,2880]{2,1,0:T(8,128)(2,1)S(1)} %bitcast.69), kind=kOutput, calls=%fused_computation.18 | convolution fusion | flops 4777574400 | bytes 14100480 | tf_op jit(solution)/shard_map/esd,efd->esf/dot_general | solution.py:67
  234.0 82.8 %all-gather.3.cloned.1.call-done = bf16[8,144,2880]{1,0,2:T(8,128)(2,1)} async-done(((bf16[8,144,720]{1,0,2:T(8,128)(2,1)}), bf16[8,144,2880]{1,0,2:T(8,128)(2,1)}) %all-gather.3.cloned.1.call-update) | async-done | bytes 6635536 | tf_op jit(solution)/shard_map/all_gather | solution.py:62
  316.9 15.4 %copy.56 = bf16[8,144,2880]{2,1,0:T(8,128)(2,1)} copy(bf16[8,144,2880]{1,0,2:T(8,128)(2,1)} %all-gather.3.cloned.1.call-done) | data formatting | bytes 13271040 | tf_op jit(solution)/shard_map/all_gather | solution.py:62
  332.2 13.6 %multiply_reduce_fusion = (f32[1152]{0:T(1024)S(1)}, bf16[1152,720]{0,1:T(8,128)(2,1)}, bf16[1152,720]{0,1:T(8,128)(2,1)S(1)}, bf16[1152,720]{0,1:T(8,128)(2,1)}) fusion(f32[1152,720]{0,1:T(8,128)} %fusion.10, f32[1152,720]{0,1:T(8,128)} %fusion.7, f32[1152]{0:T(1024)S(1)} %reshape.232, bf16[1152,2880]{1,0:T(8,128)(2,1)} %bitcast.64, ...), kind=kOutput, calls=%fused_computation.25 | convolution fusion | flops 4793332736 | bytes 22404096 | tf_op jit(solution)/shard_map/esd,efd->esf/dot_general | solution.py:72
  345.9 8.8 %fusion.5 = f32[1152,2880]{0,1:T(8,128)} fusion(bf16[1152,720]{0,1:T(8,128)(2,1)S(1)} %get-tuple-element.27, bf16[1,720,2880]{2,1,0:T(8,128)(2,1)S(1)} %bitcast.71), kind=kOutput, calls=%fused_computation.16 | convolution fusion | flops 4777574400 | bytes 19077120 | tf_op jit(solution)/shard_map/esf,efd->esd/dot_general | solution.py:81
  354.6 15.3 %fusion.1 = bf16[1,1152,2880]{1,2,0:T(8,128)(2,1)} fusion(f32[1152,2880]{0,1:T(8,128)} %fusion.5, bf16[1152,720]{0,1:T(8,128)(2,1)} %get-tuple-element.28, bf16[1,720,2880]{2,1,0:T(8,128)(2,1)} %param.12), kind=kOutput, calls=%fused_computation.10 | convolution fusion | flops 4784209920 | bytes 25712640 | tf_op jit(solution)/shard_map/esf,efd->esd/dot_general | solution.py:82
  370.0 0.0 reduce-scatter.7.cloned.1.call-update
  370.0 16.9 %psum.7 = bf16[1,1152]{1,0:T(2,128)(2,1)S(1)} all-reduce(f32[1,1152]{1,0:T(1,128)S(1)} %reduce_sum.35), channel_id=1, replica_groups=mesh['expert'=8,'hidden'=4] {'hidden'}, use_global_device_ids=true, to_apply=%region_8.9 | all-reduce | flops 1152 | bytes 6912 | tf_op jit(solution)/shard_map/psum | solution.py:85
  386.9 0.7 convert_element_type.130
  387.6 4.6 all-to-all-start.4
  392.2 11.6 %convolution_bitcast_fusion = f32[1,720,2880]{2,1,0:T(8,128)} fusion(bf16[1152,720]{0,1:T(8,128)(2,1)S(1)} %copy-done.7, bf16[1152,2880]{1,0:T(8,128)(2,1)} %bitcast.61), kind=kOutput, calls=%fused_computation.14 | convolution fusion | flops 4777574400 | bytes 16588800 | tf_op jit(solution)/shard_map/esf,esd->efd/dot_general | solution.py:80
  403.8 40.7 %reduce-scatter.7.cloned.1.call-done = bf16[1,1152,720]{1,2,0:T(8,128)(2,1)} async-done(((bf16[1,1152,2880]{1,2,0:T(8,128)(2,1)}), bf16[1,1152,720]{1,2,0:T(8,128)(2,1)}) %reduce-scatter.7.cloned.1.call-update) | async-done | bytes 1658896
  444.6 3.8 copy.59
  448.3 0.0 all-to-all-done.4
  448.4 4.6 all-to-all-start.3
  452.9 11.4 %convolution_bitcast_fusion.1 = f32[1,720,2880]{2,1,0:T(8,128)} fusion(bf16[1152,720]{0,1:T(8,128)(2,1)} %copy-done.6, bf16[1152,2880]{1,0:T(8,128)(2,1)} %bitcast.62), kind=kOutput, calls=%fused_computation.15 | convolution fusion | flops 4777574400 | bytes 16588800 | tf_op jit(solution)/shard_map/esf,esd->efd/dot_general | solution.py:79
  464.3 11.2 %fusion.4 = f32[1,720,2880]{2,1,0:T(8,128)} fusion(bf16[1152,720]{0,1:T(8,128)(2,1)S(1)} %copy-done.8, bf16[1152,2880]{1,0:T(8,128)(2,1)} %bitcast.65, f32[1152]{0:T(1024)S(1)} %reshape.232), kind=kOutput, calls=%fused_computation.13 | convolution fusion | flops 4787527680 | bytes 16593408 | tf_op jit(solution)/shard_map/esf,esd->efd/dot_general | solution.py:76
  475.6 0.1 reshape.235
  475.7 4.5 gather_fusion.4
  480.2 0.1 reshape.231
  480.3 0.7 copy.61
  480.9 14.0 %all-to-all-done.3 = bf16[8,144,720]{2,1,0:T(8,128)(2,1)S(1)} async-done(((bf16[8,144,720]{2,1,0:T(8,128)(2,1)}), bf16[8,144,720]{2,1,0:T(8,128)(2,1)S(1)}, u32[]{:S(2)}, u32[]{:S(2)}) %all-to-all-start.3) | async-done | bytes 1658912 | tf_op jit(solution)/shard_map/all_to_all | solution.py:91
  495.0 2.1 bitcast_convert_fusion
  497.1 6.1 %gather_fusion.3 = f32[768,720]{1,0:T(8,128)} fusion(f32[1152,720]{1,0:T(8,128)} %bitcast_convert_fusion, s32[1024]{0:T(1024)S(1)} %pad_clamp_fusion.2), kind=kCustom, calls=%fused_computation.3 | custom fusion | bytes 4426752 | tf_op jit(solution)/shard_map/gather | solution.py:102
  503.2 2.6 reshape.230
  505.8 2.3 reduce_sum.33
  (39 shorter events, 0.2 us)
Async XLA Ops:
  7.2 7.8 %copy-start = (bf16[192,720]{1,0:T(8,128)(2,1)S(1)}, bf16[192,720]{1,0:T(8,128)(2,1)}, u32[]{:S(2)}) copy-start(bf16[192,720]{1,0:T(8,128)(2,1)} %param.8) | copy-start | bytes 829444
  7.2 192.0 %all-gather.5.cloned.1.call-start = ((), (), s32[]{:S(2)}) async-start(), calls=%async_computation.7 | async-start | bytes 14745600 | tf_op jit(solution)/shard_map/all_gather | solution.py:61
  15.0 4.6 copy-start.2
  79.1 5.2 %copy-start.3 = (bf16[8,144,720]{2,1,0:T(8,128)(2,1)S(1)}, bf16[8,144,720]{2,1,0:T(8,128)(2,1)}, u32[]{:S(2)}) copy-start(bf16[8,144,720]{2,1,0:T(8,128)(2,1)} %get-tuple-element.31) | copy-start | bytes 4976644
  84.2 232.6 %all-gather.3.cloned.1.call-start = ((), (), s32[]{:S(2)}) async-start(), calls=%async_computation.6 | async-start | bytes 14745600 | tf_op jit(solution)/shard_map/all_gather | solution.py:62
  129.4 5.1 copy-start.5
  134.5 310.1 %reduce-scatter.7.cloned.1.call-start = ((), (), s32[]{:S(2)}) async-start(), calls=%async_computation.8 | async-start | bytes 8294400
  199.1 27.3 %slice-start = ((s8[4239360]{0:T(1024)(128)(4,1)}), s8[45056]{0:T(1024)(128)(4,1)S(1)}, s32[]{:S(2)}) async-start(s8[4239360]{0:T(1024)(128)(4,1)} %bitcast.68), calls=%async_computation.9 | async-start | bytes 90112
  215.4 11.0 %copy-start.4 = (bf16[8,144,2880]{2,1,0:T(8,128)(2,1)S(1)}, bf16[8,144,2880]{2,1,0:T(8,128)(2,1)}, u32[]{:S(2)}) copy-start(bf16[8,144,2880]{2,1,0:T(8,128)(2,1)} %copy.58) | copy-start | bytes 19906564
  215.4 11.0 %slice-start.1 = ((s8[4239360]{0:T(1024)(128)(4,1)}), s8[4194304]{0:T(1024)(128)(4,1)S(1)}, s32[]{:S(2)}) async-start(s8[4239360]{0:T(1024)(128)(4,1)} %bitcast.68), calls=%async_computation.10 | async-start | bytes 8388608
  316.9 29.0 %slice-start.2 = ((s8[4239360]{0:T(1024)(128)(4,1)}), s8[45056]{0:T(1024)(128)(4,1)S(1)}, s32[]{:S(2)}) async-start(s8[4239360]{0:T(1024)(128)(4,1)} %bitcast.70), calls=%async_computation.11 | async-start | bytes 90112
  332.2 13.6 %slice-start.3 = ((s8[4239360]{0:T(1024)(128)(4,1)}), s8[4194304]{0:T(1024)(128)(4,1)S(1)}, s32[]{:S(2)}) async-start(s8[4239360]{0:T(1024)(128)(4,1)} %bitcast.70), calls=%async_computation.12 | async-start | bytes 8388608
  345.8 8.8 %copy-start.6 = (bf16[1152,720]{0,1:T(8,128)(2,1)}, bf16[1152,720]{0,1:T(8,128)(2,1)S(1)}, u32[]{:S(2)}) copy-start(bf16[1152,720]{0,1:T(8,128)(2,1)S(1)} %get-tuple-element.27) | copy-start | bytes 4976644
  370.0 22.3 %copy-start.7 = (bf16[1152,720]{0,1:T(8,128)(2,1)S(1)}, bf16[1152,720]{0,1:T(8,128)(2,1)}, u32[]{:S(2)}) copy-start(bf16[1152,720]{0,1:T(8,128)(2,1)} %get-tuple-element.28) | copy-start | bytes 4976644
  387.6 60.7 %all-to-all-start.4 = ((bf16[8,1,144]{2,1,0:T(2,128)(2,1)}), bf16[8,1,144]{2,1,0:T(2,128)(2,1)S(1)}, u32[]{:S(2)}, u32[]{:S(2)}) async-start(bf16[8,1,144]{2,1,0:T(2,128)(2,1)} %convert_element_type.130), calls=%async_computation.4 | async-start | bytes 16384 | tf_op jit(solution)/shard_map/all_to_all | solution.py:98
  448.4 46.6 %all-to-all-start.3 = ((bf16[8,144,720]{2,1,0:T(8,128)(2,1)}), bf16[8,144,720]{2,1,0:T(8,128)(2,1)S(1)}, u32[]{:S(2)}, u32[]{:S(2)}) async-start(bf16[8,144,720]{2,1,0:T(8,128)(2,1)} %bitcast.11), calls=%async_computation.3 | async-start | bytes 3538944 | tf_op jit(solution)/shard_map/all_to_all | solution.py:91
  452.9 11.4 %copy-start.8 = (bf16[1152,720]{0,1:T(8,128)(2,1)S(1)}, bf16[1152,720]{0,1:T(8,128)(2,1)}, u32[]{:S(2)}) copy-start(bf16[1152,720]{0,1:T(8,128)(2,1)} %get-tuple-element.26) | copy-start | bytes 4976644
  497.1 11.1 %copy-start.1 = (bf16[192,720]{1,0:T(8,128)(2,1)S(1)}, bf16[192,720]{1,0:T(8,128)(2,1)}, u32[]{:S(2)}) copy-start(bf16[192,720]{1,0:T(8,128)(2,1)} %param.8) | copy-start | bytes 829444
Sparse Core Ops, SparseCore 0:
  84.3 114.7 all-gather.4
  201.0 115.8 all-gather.2
  370.1 74.3 reduce-scatter.6
where the time goes:
time: 516 us; the launch traced here: 515 us
  waiting for transfers between devices  189 us (37%)
  blocking collectives  118 us (23%)
  matrix products  90.5 us (18%)
  local copies, waits for them, and re-layouts  83.2 us (16%)
  between operations  14 us (3%)
  other arithmetic  10.2 us (2%)
  starting transfers between devices  9.32 us (2%)
    all_gather x1, waiting for transfers between devices, per_device(): lax.all_gather(got_dy, 'hidden', axis=2, tiled=True)  82.8 us
    all_gather x1, waiting for transfers between devices, per_device(): lax.all_gather(got_x, 'hidden', axis=2, tiled=True)  51.6 us
    all_to_all x1, blocking collectives, per_device(): lax.all_to_all(send_x, 'expert', split_axis=0, concat_axis=0, tiled=True)  48.3 us
    all_to_all x1, blocking collectives, per_device(): lax.all_to_all(send_dy, 'expert', split_axis=0, concat_axis=0, tiled=True)  45.2 us
    unnamed x4, waiting for transfers between devices  40.8 us
    psum x1, blocking collectives, per_device(): route_total = lax.psum(route_part, 'hidden')  16.9 us
    all_gather x1, local copies, waits for them, and re-layouts, per_device(): lax.all_gather(got_x, 'hidden', axis=2, tiled=True)  16.3 us
    all_gather x1, local copies, waits for them, and re-layouts, per_device(): lax.all_gather(got_dy, 'hidden', axis=2, tiled=True)  15.4 us
  transfers between devices with their start and end apart: 5, of which 4 were waited for; matrix products, arithmetic and copies ran while one was open for 17% of the time, Pallas kernels for 0%

commit v1 on v0

--- a/solution.py
+++ b/solution.py
@@ -2,6 +2,7 @@
 import jax.numpy as jnp
 from jax import lax
 from jax.sharding import PartitionSpec as P
+from jax.lax import all_gather
 
 
 def slot_tables(expert_ids, experts, capacity):
@@ -59,7 +60,7 @@
     )
     rows_x, rows_dy = (
         lax.all_gather(got_x, "hidden", axis=2, tiled=True),
-        lax.all_gather(got_dy, "hidden", axis=2, tiled=True),
+        jnp.concatenate(all_gather(got_dy, "hidden"), axis=2),
     )
     xs = to_local(rows_x, n_groups, local_count)
     dys = to_local(rows_dy, n_groups, local_count)

time: 516 us -> 490 us (0.950)
  waiting for transfers between devices: 189 us -> 155 us
    all_gather x1, waiting for transfers between devices: 82.8 us -> 44 us  [per_device(): all_gather(got_dy, 'hidden')]
    all_gather x1 -> x0, local copies, waits for them, and re-layouts: 15.4 us -> none  [per_device(): lax.all_gather(got_dy, 'hidden', axis=2, tiled=True)]
    another operation x1 -> x2, local copies, waits for them, and re-layouts: 0.08 us -> 13.9 us
    reshape x0 -> x1, local copies, waits for them, and re-layouts: none -> 11.4 us  [per_device(): jnp.concatenate(all_gather(got_dy, 'hidden'), axis=2)]
where the time goes in v1:
time: 490 us; the launch traced here: 484 us
  waiting for transfers between devices  155 us (32%)
  blocking collectives  119 us (24%)
  matrix products  88.6 us (18%)
  local copies, waits for them, and re-layouts  87.6 us (18%)
  between operations  14.3 us (3%)
  other arithmetic  10.2 us (2%)
  starting transfers between devices  9.52 us (2%)
    all_gather x1, waiting for transfers between devices, per_device(): lax.all_gather(got_x, 'hidden', axis=2, tiled=True)  56.4 us
    all_to_all x1, blocking collectives, per_device(): lax.all_to_all(send_x, 'expert', split_axis=0, concat_axis=0, tiled=True)  48.3 us
    all_to_all x1, blocking collectives, per_device(): lax.all_to_all(send_dy, 'expert', split_axis=0, concat_axis=0, tiled=True)  45.2 us
    all_gather x1, waiting for transfers between devices, per_device(): all_gather(got_dy, 'hidden')  44 us
    unnamed x4, waiting for transfers between devices  40.7 us
    psum x1, blocking collectives, per_device(): route_total = lax.psum(route_part, 'hidden')  16.9 us
    all_gather x1, local copies, waits for them, and re-layouts, per_device(): lax.all_gather(got_x, 'hidden', axis=2, tiled=True)  15.8 us
    all_to_all x1, waiting for transfers between devices, per_device(): lax.all_to_all(from_local(summed, n_groups, capacity).astype(jnp.bfloat16...  14 us
  transfers between devices with their start and end apart: 5, of which 4 were waited for; matrix products, arithmetic and copies ran while one was open for 17% of the time, Pallas kernels for 0%

profile of v1, /device:TPU:0, one launch (start us, length us, event | category | flops | bytes accessed | tf_op | source)
XLA Modules:
  0.0 483.7 jit_solution(3125901976314431543)
XLA Ops:
  7.2 0.0 copy-start
  7.2 0.0 all-gather.4.cloned.1.call-start
  7.2 0.7 broadcast_multiply_fusion.2
  8.0 0.8 copy.45
  8.8 0.1 eq.29
  8.9 0.1 eq.25
  9.0 0.1 copy.44
  9.1 0.1 mul.98
  9.2 1.7 reduce-window.6
  10.9 0.1 slice.18
  11.0 0.1 copy.47
  11.2 0.2 reduce-window.9
  11.3 0.1 copy.48
  11.4 0.1 fusion.15
  11.5 3.4 scatter_custom_fusion
  15.0 3.4 scatter_custom_fusion.1
  18.4 0.1 mul.102
  18.5 0.0 copy-start.2
  18.5 4.6 gather_fusion.1
  23.1 4.8 gather_fusion.2
  27.9 3.0 broadcast_multiply_fusion.1
  30.9 48.3 %all_to_all.27 = bf16[8,144,720]{2,1,0:T(8,128)(2,1)} all-to-all(bf16[8,144,720]{2,1,0:T(8,128)(2,1)S(1)} %get-tuple-element.32), channel_id=1, replica_groups=mesh['expert'=8,'hidden'=4] {'expert'}, dimensions={0} | all-to-all | bytes 3317760 | tf_op jit(solution)/shard_map/all_to_all | solution.py:55
  79.1 5.1 %copy.51 = bf16[8,144,720]{1,0,2:T(8,128)(2,1)} copy(bf16[8,144,720]{2,1,0:T(8,128)(2,1)} %all_to_all.27) | data formatting | bytes 3317760 | tf_op jit(solution)/shard_map/all_to_all | solution.py:55
  84.2 0.0 all-gather.4.cloned.1.call-update
  84.2 0.0 copy-start.5
  84.3 0.0 all-gather.6.cloned.1.call-start
  84.3 45.2 %all_to_all.28 = bf16[8,144,720]{2,1,0:T(8,128)(2,1)} all-to-all(bf16[8,144,720]{2,1,0:T(8,128)(2,1)S(1)} %copy-done.3), channel_id=1, replica_groups=mesh['expert'=8,'hidden'=4] {'expert'}, dimensions={0} | all-to-all | bytes 3317760 | tf_op jit(solution)/shard_map/all_to_all | solution.py:56
  129.5 0.0 all-gather.6.cloned.1.call-update
  129.5 0.0 reduce-scatter.7.cloned.1.call-start
  129.6 0.1 copy.43
  129.7 0.1 reshape.224
  129.8 4.6 gather_fusion
  134.4 0.1 convert_element_type.129
  134.5 8.2 %all_to_all.29 = bf16[8,1,144]{2,1,0:T(2,128)(2,1)S(1)} all-to-all(bf16[8,1,144]{2,1,0:T(2,128)(2,1)S(1)} %convert_element_type.129), channel_id=1, replica_groups=mesh['expert'=8,'hidden'=4] {'expert'}, dimensions={0} | all-to-all | bytes 4608 | tf_op jit(solution)/shard_map/all_to_all | solution.py:57
  142.7 0.1 reshape.236
  142.8 56.4 %all-gather.4.cloned.1.call-done = bf16[8,144,2880]{1,0,2:T(8,128)(2,1)} async-done(((bf16[8,144,720]{1,0,2:T(8,128)(2,1)}), bf16[8,144,2880]{1,0,2:T(8,128)(2,1)}) %all-gather.4.cloned.1.call-update) | async-done | bytes 6635536 | tf_op jit(solution)/shard_map/all_gather | solution.py:62
  199.2 15.8 %copy.52 = bf16[8,144,2880]{2,1,0:T(8,128)(2,1)} copy(bf16[8,144,2880]{1,0,2:T(8,128)(2,1)} %all-gather.4.cloned.1.call-done) | data formatting | bytes 13271040 | tf_op jit(solution)/shard_map/all_gather | solution.py:62
  215.0 11.0 %fusion.10 = f32[1152,720]{0,1:T(8,128)} fusion(bf16[1152,2880]{1,0:T(8,128)(2,1)} %bitcast.63, bf16[1,720,2880]{2,1,0:T(8,128)(2,1)} %param.12), kind=kOutput, calls=%fused_computation.21 | convolution fusion | flops 4777574400 | bytes 14100480 | tf_op jit(solution)/shard_map/esd,efd->esf/dot_general | solution.py:69
  226.0 7.6 %fusion.7 = f32[1152,720]{0,1:T(8,128)} fusion(bf16[1152,2880]{1,0:T(8,128)(2,1)S(1)} %bitcast.66, bf16[1,720,2880]{2,1,0:T(8,128)(2,1)S(1)} %bitcast.70), kind=kOutput, calls=%fused_computation.18 | convolution fusion | flops 4777574400 | bytes 14100480 | tf_op jit(solution)/shard_map/esd,efd->esf/dot_general | solution.py:68
  233.6 44.0 %all-gather.6.cloned.1.call-done = bf16[32,144,720]{2,1,0:T(8,128)(2,1)} async-done(((bf16[8,144,720]{2,1,0:T(8,128)(2,1)}), bf16[32,144,720]{2,1,0:T(8,128)(2,1)}) %all-gather.6.cloned.1.call-update) | async-done | bytes 6635536 | tf_op jit(solution)/shard_map/all_gather | solution.py:63
  277.6 11.4 %copy.50 = bf16[8,144,4,720]{3,2,1,0:T(4,128)(2,1)} copy(bf16[8,144,4,720]{3,1,0,2:T(8,128)(2,1)} %bitcast.62) | data formatting | bytes 13271040 | tf_op jit(solution)/shard_map/reshape | solution.py:63
  289.1 13.8 %reshape.227 = bf16[1152,2880]{1,0:T(8,128)(2,1)} reshape(bf16[8,144,4,720]{3,2,1,0:T(4,128)(2,1)} %copy.50) | data formatting | bytes 13271040 | tf_op jit(solution)/shard_map/reshape.4
  302.8 13.9 %multiply_reduce_fusion = (f32[1152]{0:T(1024)S(1)}, bf16[1152,720]{0,1:T(8,128)(2,1)}, bf16[1152,720]{0,1:T(8,128)(2,1)S(1)}, bf16[1152,720]{0,1:T(8,128)(2,1)S(1)}) fusion(f32[1152,720]{0,1:T(8,128)} %fusion.10, f32[1152,720]{0,1:T(8,128)} %fusion.7, f32[1152]{0:T(1024)S(1)} %reshape.236, bf16[1152,2880]{1,0:T(8,128)(2,1)} %reshape.227, ...), kind=kOutput, calls=%fused_computation.25 | convolution fusion | flops 4793332736 | bytes 22404096 | tf_op jit(solution)/shard_map/esd,efd->esf/dot_general | solution.py:73
  316.7 8.9 %fusion.5 = f32[1152,2880]{0,1:T(8,128)} fusion(bf16[1152,720]{0,1:T(8,128)(2,1)S(1)} %get-tuple-element.27, bf16[1,720,2880]{2,1,0:T(8,128)(2,1)S(1)} %bitcast.72), kind=kOutput, calls=%fused_computation.16 | convolution fusion | flops 4777574400 | bytes 19077120 | tf_op jit(solution)/shard_map/esf,efd->esd/dot_general | solution.py:82
  325.6 13.0 %fusion.1 = bf16[1,1152,2880]{1,2,0:T(8,128)(2,1)} fusion(f32[1152,2880]{0,1:T(8,128)} %fusion.5, bf16[1152,720]{0,1:T(8,128)(2,1)S(1)} %get-tuple-element.28, bf16[1,720,2880]{2,1,0:T(8,128)(2,1)} %param.12), kind=kOutput, calls=%fused_computation.10 | convolution fusion | flops 4784209920 | bytes 25712640 | tf_op jit(solution)/shard_map/esf,efd->esd/dot_general | solution.py:83
  338.7 0.0 reduce-scatter.7.cloned.1.call-update
  338.7 16.9 %psum.7 = bf16[1,1152]{1,0:T(2,128)(2,1)S(1)} all-reduce(f32[1,1152]{1,0:T(1,128)S(1)} %reduce_sum.35), channel_id=1, replica_groups=mesh['expert'=8,'hidden'=4] {'hidden'}, use_global_device_ids=true, to_apply=%region_8.9 | all-reduce | flops 1152 | bytes 6912 | tf_op jit(solution)/shard_map/psum | solution.py:86
  355.6 0.7 convert_element_type.130
  356.3 4.6 all-to-all-start.4
  360.9 11.6 %convolution_bitcast_fusion.1 = f32[1,720,2880]{2,1,0:T(8,128)} fusion(bf16[1152,720]{0,1:T(8,128)(2,1)S(1)} %copy-done.8, bf16[1152,2880]{1,0:T(8,128)(2,1)} %bitcast.64), kind=kOutput, calls=%fused_computation.15 | convolution fusion | flops 4777574400 | bytes 16588800 | tf_op jit(solution)/shard_map/esf,esd->efd/dot_general | solution.py:80
  372.5 40.7 %reduce-scatter.7.cloned.1.call-done = bf16[1,1152,720]{1,2,0:T(8,128)(2,1)} async-done(((bf16[1,1152,2880]{1,2,0:T(8,128)(2,1)}), bf16[1,1152,720]{1,2,0:T(8,128)(2,1)}) %reduce-scatter.7.cloned.1.call-update) | async-done | bytes 1658896
  413.2 3.8 copy.53
  417.1 4.8 all-to-all-start.3
  421.9 11.4 %convolution_bitcast_fusion = f32[1,720,2880]{2,1,0:T(8,128)} fusion(bf16[1152,720]{0,1:T(8,128)(2,1)} %copy-done.6, bf16[1152,2880]{1,0:T(8,128)(2,1)} %bitcast.65), kind=kOutput, calls=%fused_computation.14 | convolution fusion | flops 4777574400 | bytes 16588800 | tf_op jit(solution)/shard_map/esf,esd->efd/dot_general | solution.py:81
  433.2 11.2 %fusion.4 = f32[1,720,2880]{2,1,0:T(8,128)} fusion(bf16[1152,720]{0,1:T(8,128)(2,1)S(1)} %copy-done.9, bf16[1152,2880]{1,0:T(8,128)(2,1)} %reshape.227, f32[1152]{0:T(1024)S(1)} %reshape.236), kind=kOutput, calls=%fused_computation.13 | convolution fusion | flops 4787527680 | bytes 16593408 | tf_op jit(solution)/shard_map/esf,esd->efd/dot_general | solution.py:77
  444.5 0.1 reshape.239
  444.6 4.5 gather_fusion.4
  449.1 0.1 reshape.235
  449.2 0.7 copy.55
  449.9 14.0 %all-to-all-done.3 = bf16[8,144,720]{2,1,0:T(8,128)(2,1)S(1)} async-done(((bf16[8,144,720]{2,1,0:T(8,128)(2,1)}), bf16[8,144,720]{2,1,0:T(8,128)(2,1)S(1)}, u32[]{:S(2)}, u32[]{:S(2)}) %all-to-all-start.3) | async-done | bytes 1658912 | tf_op jit(solution)/shard_map/all_to_all | solution.py:92
  463.8 2.1 bitcast_convert_fusion
  466.0 6.1 %gather_fusion.3 = f32[768,720]{1,0:T(8,128)} fusion(f32[1152,720]{1,0:T(8,128)} %bitcast_convert_fusion, s32[1024]{0:T(1024)S(1)} %pad_clamp_fusion.2), kind=kCustom, calls=%fused_computation.3 | custom fusion | bytes 4426752 | tf_op jit(solution)/shard_map/gather | solution.py:103
  472.1 2.6 reshape.234
  474.7 2.3 reduce_sum.33
  (41 shorter events, 0.2 us)
Async XLA Ops:
  7.2 11.3 %copy-start = (bf16[192,720]{1,0:T(8,128)(2,1)S(1)}, bf16[192,720]{1,0:T(8,128)(2,1)}, u32[]{:S(2)}) copy-start(bf16[192,720]{1,0:T(8,128)(2,1)} %param.8) | copy-start | bytes 829444
  7.2 192.0 %all-gather.4.cloned.1.call-start = ((), (), s32[]{:S(2)}) async-start(), calls=%async_computation.6 | async-start | bytes 14745600 | tf_op jit(solution)/shard_map/all_gather | solution.py:62
  18.5 4.6 copy-start.2
  79.1 5.2 %copy-start.3 = (bf16[8,144,720]{2,1,0:T(8,128)(2,1)S(1)}, bf16[8,144,720]{2,1,0:T(8,128)(2,1)}, u32[]{:S(2)}) copy-start(bf16[8,144,720]{2,1,0:T(8,128)(2,1)} %get-tuple-element.31) | copy-start | bytes 4976644
  84.2 45.3 %copy-start.5 = (f32[192,4]{0,1:T(4,128)S(1)}, f32[192,4]{0,1:T(4,128)}, u32[]{:S(2)}) copy-start(f32[192,4]{0,1:T(4,128)} %param.10) | copy-start | bytes 9220
  84.3 193.4 %all-gather.6.cloned.1.call-start = ((), (), s32[]{:S(2)}) async-start(), calls=%async_computation.7 | async-start | bytes 8847360 | tf_op jit(solution)/shard_map/all_gather | solution.py:63
  129.5 283.7 %reduce-scatter.7.cloned.1.call-start = ((), (), s32[]{:S(2)}) async-start(), calls=%async_computation.8 | async-start | bytes 8294400
  199.2 26.8 %slice-start = ((s8[4239360]{0:T(1024)(128)(4,1)}), s8[45056]{0:T(1024)(128)(4,1)S(1)}, s32[]{:S(2)}) async-start(s8[4239360]{0:T(1024)(128)(4,1)} %bitcast.69), calls=%async_computation.9 | async-start | bytes 90112
  215.0 11.0 %copy-start.4 = (bf16[8,144,2880]{2,1,0:T(8,128)(2,1)S(1)}, bf16[8,144,2880]{2,1,0:T(8,128)(2,1)}, u32[]{:S(2)}) copy-start(bf16[8,144,2880]{2,1,0:T(8,128)(2,1)} %copy.52) | copy-start | bytes 19906564
  215.0 11.0 %slice-start.1 = ((s8[4239360]{0:T(1024)(128)(4,1)}), s8[4194304]{0:T(1024)(128)(4,1)S(1)}, s32[]{:S(2)}) async-start(s8[4239360]{0:T(1024)(128)(4,1)} %bitcast.69), calls=%async_computation.10 | async-start | bytes 8388608
  289.0 27.7 %slice-start.2 = ((s8[4239360]{0:T(1024)(128)(4,1)}), s8[45056]{0:T(1024)(128)(4,1)S(1)}, s32[]{:S(2)}) async-start(s8[4239360]{0:T(1024)(128)(4,1)} %bitcast.71), calls=%async_computation.11 | async-start | bytes 90112
  302.8 13.9 %slice-start.3 = ((s8[4239360]{0:T(1024)(128)(4,1)}), s8[4194304]{0:T(1024)(128)(4,1)S(1)}, s32[]{:S(2)}) async-start(s8[4239360]{0:T(1024)(128)(4,1)} %bitcast.71), calls=%async_computation.12 | async-start | bytes 8388608
  316.7 8.9 %copy-start.7 = (bf16[1152,720]{0,1:T(8,128)(2,1)}, bf16[1152,720]{0,1:T(8,128)(2,1)S(1)}, u32[]{:S(2)}) copy-start(bf16[1152,720]{0,1:T(8,128)(2,1)S(1)} %get-tuple-element.27) | copy-start | bytes 4976644
  316.7 8.9 %copy-start.6 = (bf16[1152,720]{0,1:T(8,128)(2,1)}, bf16[1152,720]{0,1:T(8,128)(2,1)S(1)}, u32[]{:S(2)}) copy-start(bf16[1152,720]{0,1:T(8,128)(2,1)S(1)} %get-tuple-element.28) | copy-start | bytes 4976644
  338.7 22.3 %copy-start.8 = (bf16[1152,720]{0,1:T(8,128)(2,1)S(1)}, bf16[1152,720]{0,1:T(8,128)(2,1)}, u32[]{:S(2)}) copy-start(bf16[1152,720]{0,1:T(8,128)(2,1)} %copy-done.7) | copy-start | bytes 4976644
  356.3 60.7 %all-to-all-start.4 = ((bf16[8,1,144]{2,1,0:T(2,128)(2,1)}), bf16[8,1,144]{2,1,0:T(2,128)(2,1)S(1)}, u32[]{:S(2)}, u32[]{:S(2)}) async-start(bf16[8,1,144]{2,1,0:T(2,128)(2,1)} %convert_element_type.130), calls=%async_computation.4 | async-start | bytes 16384 | tf_op jit(solution)/shard_map/all_to_all | solution.py:99
  417.1 46.8 %all-to-all-start.3 = ((bf16[8,144,720]{2,1,0:T(8,128)(2,1)}), bf16[8,144,720]{2,1,0:T(8,128)(2,1)S(1)}, u32[]{:S(2)}, u32[]{:S(2)}) async-start(bf16[8,144,720]{2,1,0:T(8,128)(2,1)} %bitcast.12), calls=%async_computation.3 | async-start | bytes 3538944 | tf_op jit(solution)/shard_map/all_to_all | solution.py:92
  421.9 11.4 %copy-start.9 = (bf16[1152,720]{0,1:T(8,128)(2,1)S(1)}, bf16[1152,720]{0,1:T(8,128)(2,1)}, u32[]{:S(2)}) copy-start(bf16[1152,720]{0,1:T(8,128)(2,1)} %get-tuple-element.26) | copy-start | bytes 4976644
  466.0 11.1 %copy-start.1 = (bf16[192,720]{1,0:T(8,128)(2,1)S(1)}, bf16[192,720]{1,0:T(8,128)(2,1)}, u32[]{:S(2)}) copy-start(bf16[192,720]{1,0:T(8,128)(2,1)} %param.8) | copy-start | bytes 829444
Sparse Core Ops, SparseCore 0:
  84.4 114.7 all-gather.3
  201.0 76.5 all-gather.5
  338.8 74.3 reduce-scatter.6
